TPU v7x, 32 devices: a whole 2x2x4 slice. The times are simulated.
32 devices in a mesh: section: 4 (over y, x), dp: 8 (over z, core).
Axes of the slice: x: 2, y: 2, z: 4, core: 2. Of those that a mesh axis runs over, the one named last changes fastest.
Arguments:
- saved_states: bfloat16 [4, 2, 128, 2688], P('section', None, 'dp'), may hold values from -64 to 64
- cotangent_in: bfloat16 [4, 128, 2688], P('section', 'dp'), may hold values from -6 to 6
- lengths: int32 [4], P('section'), may hold values from 16 to 128
- gain: bfloat16 [2688], replicated, may hold values from 0.099609375 to 1.8984375
- up_weight: bfloat16 [2688, 9216], P('section', 'dp'), may hold values from -0.125 to 0.125
- down_weight: bfloat16 [9216, 2688], P('dp', 'section'), may hold values from -0.0625 to 0.0625
Outputs:
- cotangent_out: bfloat16 [4, 128, 2688], P('section', 'dp')
- up_gradient: bfloat16 [2688, 9216], P('section', 'dp')
- down_gradient: bfloat16 [9216, 2688], P('dp', 'section')
- gain_gradient: float32 [2688], replicated
All inputs are finite; a program needn't handle non-finite values.
Results may differ from a plain program's by a relative error of at most 0.024.
Values may be sent and summed in bfloat16 or wider, within the bound.
No kernel may reach another device: no remote copies, remote signals or barrier semaphores. Data moves between devices by JAX's collectives and lax.ppermute only.
A program may use at most 64 MiB of HBM per device.

v0:
```python
import math
import jax
import jax.numpy as jnp
from jax import lax
from jax.sharding import PartitionSpec as P

epsilon = 1e-06


def passed_along(block, axis, distance):
    devices = range(lax.axis_size(axis))
    route = [((i - distance) % len(devices), i) for i in devices]
    return lax.ppermute(block, axis, route)


def back_iteration(state, cotangent, gain, up_full, down_full, member, share):
    values = state.astype(jnp.float32)
    reciprocal = lax.rsqrt(jnp.mean(values * values, axis=-1, keepdims=True) + epsilon)
    scaled = values * reciprocal
    gain_wide = gain.astype(jnp.float32)
    normed = (scaled * gain_wide).astype(jnp.bfloat16)
    hidden_in = jnp.dot(normed, up_full, preferred_element_type=jnp.float32)
    sigma = jax.nn.sigmoid(hidden_in)
    hidden_out = (hidden_in * sigma).astype(jnp.bfloat16)
    back_out = lax.dot_general(
        cotangent, down_full, (((1,), (1,)), ((), ())), preferred_element_type=jnp.float32
    )
    back_in = (back_out * sigma * (1.0 + hidden_in * (1.0 - sigma))).astype(jnp.bfloat16)
    partial_value = lax.dot_general(
        back_in, up_full, (((1,), (1,)), ((), ())), preferred_element_type=jnp.float32
    )
    back_normed = lax.psum_scatter(
        partial_value.astype(jnp.bfloat16), "dp", scatter_dimension=0, tiled=True
    ).astype(jnp.float32)
    start = member * share
    rows_scaled = lax.dynamic_slice_in_dim(scaled, start, share, 0)
    rows_recip = lax.dynamic_slice_in_dim(reciprocal, start, share, 0)
    rows_cot = lax.dynamic_slice_in_dim(cotangent, start, share, 0)
    gained = back_normed * gain_wide
    back_state = rows_recip * (
        gained - rows_scaled * jnp.mean(gained * rows_scaled, axis=-1, keepdims=True)
    )
    result = (rows_cot.astype(jnp.float32) + back_state).astype(jnp.bfloat16)
    gain_term = jnp.sum(back_normed * rows_scaled, axis=0)
    return (result, normed, back_in, hidden_out, gain_term)


def hand_over(result):
    arrived = passed_along(result, "section", -1)
    return lax.all_gather(arrived, "dp", axis=0, tiled=True)


def contract_rows(left, right):
    return lax.dot_general(
        left, right, (((0,), (0,)), ((), ())), preferred_element_type=jnp.float32
    )


def reduce_terms(up_terms, down_terms):
    return (
        lax.psum_scatter(
            up_terms.astype(jnp.bfloat16), "section", scatter_dimension=0, tiled=True
        ).astype(jnp.float32),
        lax.psum_scatter(
            down_terms.astype(jnp.bfloat16), "section", scatter_dimension=1, tiled=True
        ).astype(jnp.float32),
    )


def on_device(saved_states, cotangent_in, lengths, gain, up_weight, down_weight):
    up_full, down_full = (
        lax.all_gather(up_weight, "section", axis=0, tiled=True),
        lax.all_gather(down_weight, "section", axis=1, tiled=True),
    )
    group_states, group_cotangent = (
        lax.all_gather(saved_states, "dp", axis=2, tiled=True),
        lax.all_gather(cotangent_in, "dp", axis=1, tiled=True),
    )
    turns = group_states.shape[1]
    tokens = group_states.shape[2]
    share = saved_states.shape[2]
    member = lax.axis_index("dp")
    positions = lax.broadcasted_iota(jnp.int32, (tokens, 1), 0)
    cotangent = jnp.where(
        positions < lengths[0], group_cotangent[0], jnp.zeros_like(group_cotangent[0])
    )
    scale = 1.0 / math.sqrt(turns * tokens * lax.axis_size("section"))
    gain_total = jnp.zeros((gain.shape[0],), jnp.float32)
    up_total = jnp.zeros(up_full.shape, jnp.float32)
    down_total = jnp.zeros(down_full.shape, jnp.float32)
    result = cotangent
    for turn in range(turns):
        if turn > 0:
            cotangent = hand_over(result)
        result, normed, back_in, hidden_out, gain_term = back_iteration(
            group_states[0, turn], cotangent, gain, up_full, down_full, member, share
        )
        gain_total = gain_total + gain_term
        up_total = up_total + contract_rows(normed, back_in)
        down_total = down_total + contract_rows(hidden_out, cotangent)
    up_sum, down_sum = reduce_terms(up_total * scale, down_total * scale)
    gain_sum = lax.psum(gain_total * scale, ("section", "dp"))
    own_rows = result[None]
    return (own_rows, up_sum.astype(jnp.bfloat16), down_sum.astype(jnp.bfloat16), gain_sum)


def solution(mesh):
    placed = (
        P("section", None, "dp", None),
        P("section", "dp", None),
        P("section"),
        P(),
        P("section", "dp"),
        P("dp", "section"),
    )
    return jax.shard_map(
        on_device,
        mesh=mesh,
        in_specs=placed,
        out_specs=(P("section", "dp", None), P("section", "dp"), P("dp", "section"), P()),
        check_vma=False,
    )
```

profile of v0, /device:TPU:0, one launch (start us, length us, event | category | flops | bytes accessed | tf_op | source)
XLA Modules:
  0.0 431.3 jit_solution(11454074368772299027)
XLA Ops:
  7.2 0.0 all-gather.4.cloned.1.call-start
  7.2 0.7 all-gather.4.cloned.1.call-update
  7.9 0.0 all-gather.8.cloned.1.call-start
  8.0 0.7 all-gather.8.cloned.1.call-update
  8.7 0.0 all-gather.6.cloned.1.call-start
  8.7 0.7 all-gather.6.cloned.1.call-update
  9.4 0.0 reduce-scatter.5.cloned.1.call-start
  10.1 18.4 %all_gather.15 = bf16[1,128,2688]{2,1,0:T(8,128)(2,1)S(1)} all-gather(bf16[1,16,2688]{2,1,0:T(8,128)(2,1)S(1)} %copy-done.5), channel_id=1, replica_groups=mesh['section'=4,'dp'=8] {'dp'}, dimensions={1}, use_global_device_ids=true | all-gather | bytes 774144 | tf_op jit(solution)/shard_map/all_gather | solution.py:77
  28.5 0.1 bitcast_select_fusion
  28.7 8.8 %all-gather.4.cloned.1.call-done = bf16[1,2,128,2688]{3,2,1,0:T(8,128)(2,1)} async-done(((bf16[1,2,16,2688]{3,2,1,0:T(8,128)(2,1)}), bf16[1,2,128,2688]{3,2,1,0:T(8,128)(2,1)}) %all-gather.4.cloned.1.call-update) | async-done | bytes 1376272 | tf_op jit(solution)/shard_map/all_gather | solution.py:76
  37.4 1.8 fusion.8
  39.2 68.8 %all-gather.8.cloned.1.call-done = bf16[2688,1152]{1,0:T(8,128)(2,1)} async-done(((bf16[672,1152]{1,0:T(8,128)(2,1)}), bf16[2688,1152]{1,0:T(8,128)(2,1)}) %all-gather.8.cloned.1.call-update) | async-done | bytes 6193168 | tf_op jit(solution)/shard_map/all_gather | solution.py:72
  108.0 3.9 fusion.14
  111.9 67.2 %all-gather.6.cloned.1.call-done = bf16[1152,2688]{0,1:T(8,128)(2,1)} async-done(((bf16[1152,672]{0,1:T(8,128)(2,1)}), bf16[1152,2688]{0,1:T(8,128)(2,1)}) %all-gather.6.cloned.1.call-update) | async-done | bytes 6193168 | tf_op jit(solution)/shard_map/all_gather | solution.py:73
  179.1 4.1 fusion.6
  183.2 0.5 copy-done
  183.7 2.8 convolution_convert_fusion.1
  186.4 0.0 reduce-scatter.5.cloned.1.call-update
  186.5 0.0 reduce-scatter.7.cloned.1.call-start
  186.5 0.1 dynamic-slice.6
  186.6 1.8 convert_multiply_fusion.2
  188.4 30.0 %reduce-scatter.5.cloned.1.call-done = bf16[16,2688]{1,0:T(8,128)(2,1)} async-done(((bf16[128,2688]{1,0:T(8,128)(2,1)}), bf16[16,2688]{1,0:T(8,128)(2,1)}) %reduce-scatter.5.cloned.1.call-update) | async-done | bytes 86032 | tf_op jit(solution)/shard_map/reduce_scatter | solution.py:32
  218.4 1.6 fusion.28
  220.0 1.1 fusion.27
  221.1 2.4 collective-permute-start
  223.5 4.1 fusion.15
  227.5 15.4 %all_gather.19 = bf16[128,2688]{1,0:T(8,128)(2,1)S(1)} all-gather(bf16[16,2688]{1,0:T(8,128)(2,1)S(1)} %collective-permute-done), channel_id=1, replica_groups=mesh['section'=4,'dp'=8] {'dp'}, dimensions={0}, use_global_device_ids=true | all-gather | bytes 774144 | tf_op jit(solution)/shard_map/all_gather | solution.py:50
  243.0 4.1 fusion.7
  247.1 0.0 copy-start.3
  247.1 0.7 copy-done.3
  247.8 2.8 convolution_convert_fusion
  250.6 0.0 reduce-scatter.7.cloned.1.call-update
  250.6 0.2 reduce-scatter.11.cloned.1.call-start
  250.8 2.9 fusion.10
  253.8 4.6 %fusion.2 = bf16[1152,2688]{0,1:T(8,128)(2,1)} fusion(f32[1152,2688]{0,1:T(8,128)S(1)} %fusion.10, bf16[128,2688]{1,0:T(8,128)(2,1)S(1)} %all_gather.19, f32[128,1152]{1,0:T(8,128)S(1)} %fusion.15), kind=kOutput, calls=%fused_computation.4 | convolution fusion | flops 802750464 | bytes 19857408 | tf_op jit(solution)/shard_map/dot_general | solution.py:54
  258.3 0.0 reduce-scatter.11.cloned.1.call-update
  258.4 0.0 copy-start.4
  258.4 0.0 reduce-scatter.9.cloned.1.call-start
  258.4 1.9 fusion.13
  260.3 4.5 %fusion.3 = bf16[2688,1152]{1,0:T(8,128)(2,1)} fusion(f32[2688,1152]{1,0:T(8,128)S(1)} %fusion.13, bf16[128,1152]{1,0:T(8,128)(2,1)S(1)} %copy-done.4, f32[2688]{0:T(1024)S(1)} %convert_element_type.71, f32[128]{0:T(128)S(1)} %copy-done.9, bf16[1,2,128,2688]{3,2,1,0:T(8,128)(2,1)S(1)} %copy-done.1), kind=kOutput, calls=%fused_computation.5 | convolution fusion | flops 803389440 | bytes 19575296 | tf_op jit(solution)/shard_map/dot_general | solution.py:54
  264.9 0.0 reduce-scatter.9.cloned.1.call-update
  264.9 0.1 dynamic-slice.7
  265.0 14.7 %reduce-scatter.7.cloned.1.call-done = bf16[16,2688]{1,0:T(8,128)(2,1)} async-done(((bf16[128,2688]{1,0:T(8,128)(2,1)}), bf16[16,2688]{1,0:T(8,128)(2,1)}) %reduce-scatter.7.cloned.1.call-update) | async-done | bytes 86032 | tf_op jit(solution)/shard_map/reduce_scatter | solution.py:32
  279.7 1.1 fusion.29
  280.9 38.9 %psum.7 = f32[2688]{0:T(1024)} all-reduce(f32[2688]{0:T(1024)S(1)} %add_multiply_fusion), channel_id=1, replica_groups=mesh['section'=4,'dp'=8] {'section','dp'}, use_global_device_ids=true, to_apply=%region_10.11 | all-reduce | flops 2688 | bytes 21504 | tf_op jit(solution)/shard_map/psum | solution.py:102
  319.8 1.7 fusion.30
  321.5 30.1 %reduce-scatter.11.cloned.1.call-done = bf16[1152,672]{0,1:T(8,128)(2,1)} async-done(((bf16[1152,2688]{0,1:T(8,128)(2,1)}), bf16[1152,672]{0,1:T(8,128)(2,1)}) %reduce-scatter.11.cloned.1.call-update) | async-done | bytes 1548304 | tf_op jit(solution)/shard_map/reduce_scatter | solution.py:64
  351.5 72.9 %reduce-scatter.9.cloned.1.call-done = bf16[672,1152]{1,0:T(8,128)(2,1)} async-done(((bf16[2688,1152]{1,0:T(8,128)(2,1)}), bf16[672,1152]{1,0:T(8,128)(2,1)}) %reduce-scatter.9.cloned.1.call-update) | async-done | bytes 1548304 | tf_op jit(solution)/shard_map/reduce_scatter | solution.py:61
  (29 shorter events, 0.1 us)
Async XLA Ops:
  7.2 30.3 %all-gather.4.cloned.1.call-start = ((), (), s32[]{:S(2)}) async-start(), calls=%async_computation.4 | async-start | bytes 1548288 | tf_op jit(solution)/shard_map/all_gather | solution.py:76
  7.9 2.2 copy-start.7
  7.9 2.2 copy-start.5
  7.9 100.1 %all-gather.8.cloned.1.call-start = ((), (), s32[]{:S(2)}) async-start(), calls=%async_computation.6 | async-start | bytes 7741440 | tf_op jit(solution)/shard_map/all_gather | solution.py:72
  8.7 170.4 %all-gather.6.cloned.1.call-start = ((), (), s32[]{:S(2)}) async-start(), calls=%async_computation.5 | async-start | bytes 7741440 | tf_op jit(solution)/shard_map/all_gather | solution.py:73
  9.4 209.0 %reduce-scatter.5.cloned.1.call-start = ((), (), s32[]{:S(2)}) async-start(), calls=%async_computation.7 | async-start | bytes 774144 | tf_op jit(solution)/shard_map/reduce_scatter | solution.py:32
  28.7 191.3 %copy-start.2 = (bf16[128,2688]{1,0:T(8,128)(2,1)}, bf16[128,2688]{1,0:T(8,128)(2,1)S(1)}, u32[]{:S(2)}) copy-start(bf16[128,2688]{1,0:T(8,128)(2,1)S(1)} %bitcast_select_fusion) | copy-start | bytes 2064388
  37.4 70.6 %copy-start.1 = (bf16[1,2,128,2688]{3,2,1,0:T(8,128)(2,1)S(1)}, bf16[1,2,128,2688]{3,2,1,0:T(8,128)(2,1)}, u32[]{:S(2)}) copy-start(bf16[1,2,128,2688]{3,2,1,0:T(8,128)(2,1)} %all-gather.4.cloned.1.call-done) | copy-start | bytes 4128772
  179.1 4.5 %copy-start = (bf16[2688,1152]{1,0:T(8,128)(2,1)S(1)}, bf16[2688,1152]{1,0:T(8,128)(2,1)}, u32[]{:S(2)}) copy-start(bf16[2688,1152]{1,0:T(8,128)(2,1)} %all-gather.8.cloned.1.call-done) | copy-start | bytes 18579460
  186.5 93.3 %reduce-scatter.7.cloned.1.call-start = ((), (), s32[]{:S(2)}) async-start(), calls=%async_computation.8 | async-start | bytes 774144 | tf_op jit(solution)/shard_map/reduce_scatter | solution.py:32
  186.6 1.8 copy-start.8
  221.1 6.5 %collective-permute-start = (bf16[16,2688]{1,0:T(8,128)(2,1)S(1)}, bf16[16,2688]{1,0:T(8,128)(2,1)S(1)}, u32[]{:S(2)}, u32[]{:S(2)}) collective-permute-start(bf16[16,2688]{1,0:T(8,128)(2,1)S(1)} %fusion.27), channel_id=1, source_target_pairs={{8,0},{16,8},{24,16},{0,24},{9,1},{17,9},{25,17},{1,25},{10,2},{18... | collective-permute-start | bytes 258056 | tf_op jit(solution)/shard_map/ppermute | solution.py:13
  223.5 24.3 %slice-start = ((s8[6193152]{0:T(1024)(128)(4,1)}), s8[4194304]{0:T(1024)(128)(4,1)S(1)}, s32[]{:S(2)}) async-start(s8[6193152]{0:T(1024)(128)(4,1)} %bitcast.46), calls=%async_computation.11 | async-start | bytes 8388608
  243.0 4.8 %slice-start.1 = ((s8[6193152]{0:T(1024)(128)(4,1)}), s8[1998848]{0:T(1024)(128)(4,1)S(1)}, s32[]{:S(2)}) async-start(s8[6193152]{0:T(1024)(128)(4,1)} %bitcast.46), calls=%async_computation.12 | async-start | bytes 3997696
  247.1 0.7 copy-start.3
  250.6 100.9 %reduce-scatter.11.cloned.1.call-start = ((), (), s32[]{:S(2)}) async-start(), calls=%async_computation.10 | async-start | bytes 7741440 | tf_op jit(solution)/shard_map/reduce_scatter | solution.py:64
  258.4 2.0 copy-start.4
  258.4 2.0 copy-start.9
  258.4 166.1 %reduce-scatter.9.cloned.1.call-start = ((), (), s32[]{:S(2)}) async-start(), calls=%async_computation.9 | async-start | bytes 7741440 | tf_op jit(solution)/shard_map/reduce_scatter | solution.py:61
  264.9 16.0 %copy-start.6 = (f32[2688]{0:T(1024)S(1)}, f32[2688]{0:T(1024)}, u32[]{:S(2)}) copy-start(f32[2688]{0:T(1024)} %get-tuple-element.6) | copy-start | bytes 32260
Sparse Core Ops, SparseCore 0:
  9.6 27.8 all-gather.3
  39.3 68.6 all-gather.7
  109.9 69.1 all-gather.5
  186.6 31.7 reduce-scatter.4
  250.7 28.9 reduce-scatter.6
  283.2 68.2 reduce-scatter.10
  355.2 69.2 reduce-scatter.8
where the time goes:
time: 432 us; the launch traced here: 431 us
  waiting for transfers between devices  295 us (68%)
  blocking collectives  72.7 us (17%)
  matrix products  35.6 us (8%)
  between operations  14.9 us (3%)
  other arithmetic  9.26 us (2%)
    reduce_scatter x1, waiting for transfers between devices, reduce_terms(): lax.psum_scatter(up_terms.astype(jnp.bfloat16), 'section', scatter_dimens...  72.9 us
    all_gather x1, waiting for transfers between devices, on_device(): lax.all_gather(up_weight, 'section', axis=0, tiled=True)  68.8 us
    all_gather x1, waiting for transfers between devices, on_device(): lax.all_gather(down_weight, 'section', axis=1, tiled=True)  67.2 us
    reduce_scatter x2, waiting for transfers between devices, back_iteration(): lax.psum_scatter(partial_value.astype(jnp.bfloat16), 'dp', scatter_dimens...  44.7 us
    psum x1, blocking collectives, on_device(): gain_sum = lax.psum(gain_total * scale, ('section', 'dp'))  38.9 us
    reduce_scatter x1, waiting for transfers between devices, reduce_terms(): lax.psum_scatter(down_terms.astype(jnp.bfloat16), 'section', scatter_dime...  30.1 us
    all_gather x1, blocking collectives, on_device(): lax.all_gather(cotangent_in, 'dp', axis=1, tiled=True)  18.4 us
    all_gather x1, blocking collectives, hand_over(): return lax.all_gather(arrived, 'dp', axis=0, tiled=True)  15.4 us
  transfers between devices with their start and end apart: 8, of which 7 were waited for; matrix products, arithmetic and copies ran while one was open for 7% of the time, Pallas kernels for 0%

commit v1 on v0

--- a/solution.py
+++ b/solution.py
@@ -69,7 +69,10 @@
 
 def on_device(saved_states, cotangent_in, lengths, gain, up_weight, down_weight):
     up_full, down_full = (
-        lax.all_gather(up_weight, "section", axis=0, tiled=True),
+        jnp.concatenate(
+            lax.all_to_all(jnp.stack([up_weight] * lax.axis_size("section")), "section", 0, 0),
+            axis=0,
+        ),
         lax.all_gather(down_weight, "section", axis=1, tiled=True),
     )
     group_states, group_cotangent = (

time: 432 us -> 403 us (0.933)
  waiting for transfers between devices: 295 us -> 249 us
  starting transfers between devices: 2.84 us -> 8.28 us
  local copies, waits for them, and re-layouts: 1.37 us -> 6.09 us
    all_gather x1 -> x0, waiting for transfers between devices: 68.8 us -> none  [on_device(): lax.all_gather(up_weight, 'section', axis=0, tiled=True)]
    all_to_all x0 -> x1, waiting for transfers between devices: none -> 60.6 us  [on_device(): lax.all_to_all(jnp.stack([up_weight] * lax.axis_size('section')), 'sectio...]
    reduce_scatter x1, waiting for transfers between devices: 72.9 us -> 30.1 us  [reduce_terms(): lax.psum_scatter(up_terms.astype(jnp.bfloat16), 'section', scatter_dimens...]
    reduce_scatter x1, waiting for transfers between devices: 30.1 us -> 72.8 us  [reduce_terms(): lax.psum_scatter(down_terms.astype(jnp.bfloat16), 'section', scatter_dime...]
    all_gather x1, waiting for transfers between devices: 67.2 us -> 37.5 us  [on_device(): lax.all_gather(down_weight, 'section', axis=1, tiled=True)]
    all_gather x1, waiting for transfers between devices: 8.75 us -> 2.39 us  [on_device(): lax.all_gather(saved_states, 'dp', axis=2, tiled=True)]
    dot_general x2, matrix products: 5.59 us -> 11.1 us  [back_iteration(): lax.dot_general(back_in, up_full, (((1,), (1,)), ((), ())), preferred_ele...]
    all_to_all x0 -> x1, starting transfers between devices: none -> 5.37 us  [on_device(): lax.all_to_all(jnp.stack([up_weight] * lax.axis_size('section')), 'sectio...]
  transfers between devices with their start and end apart: 8 -> 8, of which waited for: 7 -> 7; matrix products, arithmetic and copies ran while one was open for 7% -> 8% of each run, Pallas kernels for 0% -> 0%
where the time goes in v1:
time: 403 us
  waiting for transfers between devices  249 us (62%)
  blocking collectives  75.6 us (19%)
  matrix products  39.6 us (10%)
  between operations  14.9 us (4%)
  other arithmetic  9.22 us (2%)
  starting transfers between devices  8.28 us (2%)
  local copies, waits for them, and re-layouts  6.09 us (2%)
    reduce_scatter x1, waiting for transfers between devices, reduce_terms(): lax.psum_scatter(down_terms.astype(jnp.bfloat16), 'section', scatter_dime...  72.8 us
    all_to_all x1, waiting for transfers between devices, on_device(): lax.all_to_all(jnp.stack([up_weight] * lax.axis_size('section')), 'sectio...  60.6 us
    reduce_scatter x2, waiting for transfers between devices, back_iteration(): lax.psum_scatter(partial_value.astype(jnp.bfloat16), 'dp', scatter_dimens...  44.1 us
    psum x1, blocking collectives, on_device(): gain_sum = lax.psum(gain_total * scale, ('section', 'dp'))  38.9 us
    all_gather x1, waiting for transfers between devices, on_device(): lax.all_gather(down_weight, 'section', axis=1, tiled=True)  37.5 us
    reduce_scatter x1, waiting for transfers between devices, reduce_terms(): lax.psum_scatter(up_terms.astype(jnp.bfloat16), 'section', scatter_dimens...  30.1 us
    all_gather x1, blocking collectives, on_device(): lax.all_gather(cotangent_in, 'dp', axis=1, tiled=True)  21.3 us
    all_gather x1, blocking collectives, hand_over(): return lax.all_gather(arrived, 'dp', axis=0, tiled=True)  15.4 us
  transfers between devices with their start and end apart: 8, of which 7 were waited for; matrix products, arithmetic and copies ran while one was open for 8% of the time, Pallas kernels for 0%

profile of v1, /device:TPU:0, one launch (start us, length us, event | category | flops | bytes accessed | tf_op | source)
XLA Modules:
  0.0 402.5 jit_solution(16659409004208462910)
XLA Ops:
  7.2 0.0 all-gather.3.cloned.1.call-start
  7.2 0.7 all-gather.3.cloned.1.call-update
  7.9 0.0 all-gather.5.cloned.1.call-start
  8.0 0.7 all-gather.5.cloned.1.call-update
  8.7 3.0 stack.2
  11.7 5.4 %all-to-all-start = ((bf16[4,672,1152]{2,1,0:T(8,128)(2,1)}), bf16[4,672,1152]{2,1,0:T(8,128)(2,1)}, u32[]{:S(2)}, u32[]{:S(2)}) async-start(bf16[4,672,1152]{2,1,0:T(8,128)(2,1)} %stack.2), calls=%async_computation | async-start | bytes 12386304 | tf_op jit(solution)/shard_map/all_to_all | solution.py:73
  17.1 0.0 reduce-scatter.5.cloned.1.call-start
  17.8 21.3 %all_gather.12 = bf16[1,128,2688]{2,1,0:T(8,128)(2,1)S(1)} all-gather(bf16[1,16,2688]{2,1,0:T(8,128)(2,1)S(1)} %copy-done.6), channel_id=1, replica_groups=mesh['section'=4,'dp'=8] {'dp'}, dimensions={1}, use_global_device_ids=true | all-gather | bytes 774144 | tf_op jit(solution)/shard_map/all_gather | solution.py:80
  39.1 0.1 bitcast_select_fusion
  39.2 2.4 all-gather.3.cloned.1.call-done
  41.6 1.8 fusion.12
  43.4 60.6 %all-to-all-done = bf16[4,672,1152]{2,1,0:T(8,128)(2,1)} async-done(((bf16[4,672,1152]{2,1,0:T(8,128)(2,1)}), bf16[4,672,1152]{2,1,0:T(8,128)(2,1)}, u32[]{:S(2)}, u32[]{:S(2)}) %all-to-all-start) | async-done | bytes 6193184 | tf_op jit(solution)/shard_map/all_to_all | solution.py:73
  104.0 3.9 fusion.23
  107.9 37.5 %all-gather.5.cloned.1.call-done = bf16[1152,2688]{0,1:T(8,128)(2,1)} async-done(((bf16[1152,672]{0,1:T(8,128)(2,1)}), bf16[1152,2688]{0,1:T(8,128)(2,1)}) %all-gather.5.cloned.1.call-update) | async-done | bytes 6193168 | tf_op jit(solution)/shard_map/all_gather | solution.py:76
  145.4 3.9 fusion.6
  149.4 5.5 %convolution_convert_fusion.1 = bf16[128,2688]{1,0:T(8,128)(2,1)} fusion(bf16[128,1152]{1,0:T(8,128)(2,1)S(1)} %fusion.6, bf16[2688,1152]{1,0:T(8,128)(2,1)} %bitcast.4), kind=kOutput, calls=%fused_computation.7 | convolution fusion | flops 793067520 | bytes 7176192 | tf_op jit(solution)/shard_map/dot_general | solution.py:29
  154.9 0.0 reduce-scatter.5.cloned.1.call-update
  154.9 0.0 reduce-scatter.7.cloned.1.call-start
  155.0 0.1 dynamic-slice.6
  155.1 0.5 copy-done.9
  155.6 1.8 fusion.10
  157.3 29.5 %reduce-scatter.5.cloned.1.call-done = bf16[16,2688]{1,0:T(8,128)(2,1)} async-done(((bf16[128,2688]{1,0:T(8,128)(2,1)}), bf16[16,2688]{1,0:T(8,128)(2,1)}) %reduce-scatter.5.cloned.1.call-update) | async-done | bytes 86032 | tf_op jit(solution)/shard_map/reduce_scatter | solution.py:32
  186.8 1.6 fusion.48
  188.5 1.1 fusion.47
  189.5 2.5 collective-permute-start
  192.0 3.9 fusion.20
  196.0 15.4 %all_gather.15 = bf16[128,2688]{1,0:T(8,128)(2,1)S(1)} all-gather(bf16[16,2688]{1,0:T(8,128)(2,1)S(1)} %collective-permute-done), channel_id=1, replica_groups=mesh['section'=4,'dp'=8] {'dp'}, dimensions={0}, use_global_device_ids=true | all-gather | bytes 774144 | tf_op jit(solution)/shard_map/all_gather | solution.py:50
  211.4 3.9 fusion.7
  215.3 0.7 copy-done.4
  216.0 5.6 %convolution_convert_fusion = bf16[128,2688]{1,0:T(8,128)(2,1)} fusion(bf16[128,1152]{1,0:T(8,128)(2,1)S(1)} %fusion.7, bf16[2688,1152]{1,0:T(8,128)(2,1)} %bitcast.4), kind=kOutput, calls=%fused_computation.6 | convolution fusion | flops 793067520 | bytes 7176192 | tf_op jit(solution)/shard_map/dot_general | solution.py:29
  221.6 0.0 reduce-scatter.7.cloned.1.call-update
  221.6 0.2 reduce-scatter.9.cloned.1.call-start
  221.9 1.9 fusion.18
  223.8 4.5 %fusion.3 = bf16[2688,1152]{1,0:T(8,128)(2,1)} fusion(f32[2688,1152]{1,0:T(8,128)S(1)} %fusion.18, bf16[128,1152]{1,0:T(8,128)(2,1)S(1)} %copy-done.5, f32[2688]{0:T(1024)S(1)} %convert_element_type.88, f32[128]{0:T(128)S(1)} %copy-done.10, bf16[1,2,128,2688]{3,2,1,0:T(8,128)(2,1)S(1)} %copy-done), kind=kOutput, calls=%fused_computation.5 | convolution fusion | flops 803389440 | bytes 19575296 | tf_op jit(solution)/shard_map/dot_general | solution.py:54
  228.3 0.0 reduce-scatter.9.cloned.1.call-update
  228.4 0.0 reduce-scatter.11.cloned.1.call-start
  228.4 1.0 copy-done.2
  229.4 1.8 fusion.33
  231.3 4.5 %fusion.2 = bf16[1152,2688]{0,1:T(8,128)(2,1)} fusion(f32[1152,2688]{0,1:T(8,128)S(1)} %fusion.33, bf16[128,2688]{1,0:T(8,128)(2,1)S(1)} %all_gather.15, f32[128,1152]{1,0:T(8,128)S(1)} %fusion.20), kind=kOutput, calls=%fused_computation.4 | convolution fusion | flops 802750464 | bytes 19857408 | tf_op jit(solution)/shard_map/dot_general | solution.py:54
  235.8 0.0 reduce-scatter.11.cloned.1.call-update
  235.8 0.6 copy-done.11
  236.5 0.1 dynamic-slice.7
  236.5 14.6 %reduce-scatter.7.cloned.1.call-done = bf16[16,2688]{1,0:T(8,128)(2,1)} async-done(((bf16[128,2688]{1,0:T(8,128)(2,1)}), bf16[16,2688]{1,0:T(8,128)(2,1)}) %reduce-scatter.7.cloned.1.call-update) | async-done | bytes 86032 | tf_op jit(solution)/shard_map/reduce_scatter | solution.py:32
  251.1 1.1 fusion.49
  252.2 38.9 %psum.7 = f32[2688]{0:T(1024)} all-reduce(f32[2688]{0:T(1024)S(1)} %add_multiply_fusion), channel_id=1, replica_groups=mesh['section'=4,'dp'=8] {'section','dp'}, use_global_device_ids=true, to_apply=%region_10.11 | all-reduce | flops 2688 | bytes 21504 | tf_op jit(solution)/shard_map/psum | solution.py:105
  291.1 1.7 fusion.50
  292.8 30.1 %reduce-scatter.9.cloned.1.call-done = bf16[672,1152]{1,0:T(8,128)(2,1)} async-done(((bf16[2688,1152]{1,0:T(8,128)(2,1)}), bf16[672,1152]{1,0:T(8,128)(2,1)}) %reduce-scatter.9.cloned.1.call-update) | async-done | bytes 1548304 | tf_op jit(solution)/shard_map/reduce_scatter | solution.py:61
  322.9 72.8 %reduce-scatter.11.cloned.1.call-done = bf16[1152,672]{0,1:T(8,128)(2,1)} async-done(((bf16[1152,2688]{0,1:T(8,128)(2,1)}), bf16[1152,672]{0,1:T(8,128)(2,1)}) %reduce-scatter.11.cloned.1.call-update) | async-done | bytes 1548304 | tf_op jit(solution)/shard_map/reduce_scatter | solution.py:64
  (28 shorter events, 0.1 us)
Async XLA Ops:
  7.2 1.5 copy-start.3
  7.2 34.5 %all-gather.3.cloned.1.call-start = ((), (), s32[]{:S(2)}) async-start(), calls=%async_computation.5 | async-start | bytes 1548288 | tf_op jit(solution)/shard_map/all_gather | solution.py:79
  7.9 137.5 %all-gather.5.cloned.1.call-start = ((), (), s32[]{:S(2)}) async-start(), calls=%async_computation.6 | async-start | bytes 7741440 | tf_op jit(solution)/shard_map/all_gather | solution.py:76
  11.7 6.1 %copy-start.8 = (bf16[2688]{0:T(1024)(128)(2,1)S(1)}, bf16[2688]{0:T(1024)(128)(2,1)}, u32[]{:S(2)}) copy-start(bf16[2688]{0:T(1024)(128)(2,1)} %param.9) | copy-start | bytes 16132
  11.7 6.1 %copy-start.6 = (bf16[1,16,2688]{2,1,0:T(8,128)(2,1)S(1)}, bf16[1,16,2688]{2,1,0:T(8,128)(2,1)}, u32[]{:S(2)}) copy-start(bf16[1,16,2688]{2,1,0:T(8,128)(2,1)} %param.7) | copy-start | bytes 258052
  11.7 92.3 %all-to-all-start = ((bf16[4,672,1152]{2,1,0:T(8,128)(2,1)}), bf16[4,672,1152]{2,1,0:T(8,128)(2,1)}, u32[]{:S(2)}, u32[]{:S(2)}) async-start(bf16[4,672,1152]{2,1,0:T(8,128)(2,1)} %stack.2), calls=%async_computation | async-start | bytes 12386304 | tf_op jit(solution)/shard_map/all_to_all | solution.py:73
  17.1 169.8 %reduce-scatter.5.cloned.1.call-start = ((), (), s32[]{:S(2)}) async-start(), calls=%async_computation.7 | async-start | bytes 774144 | tf_op jit(solution)/shard_map/reduce_scatter | solution.py:32
  39.2 149.2 %copy-start.1 = (bf16[128,2688]{1,0:T(8,128)(2,1)}, bf16[128,2688]{1,0:T(8,128)(2,1)S(1)}, u32[]{:S(2)}) copy-start(bf16[128,2688]{1,0:T(8,128)(2,1)S(1)} %bitcast_select_fusion) | copy-start | bytes 2064388
  41.6 62.3 %copy-start = (bf16[1,2,128,2688]{3,2,1,0:T(8,128)(2,1)S(1)}, bf16[1,2,128,2688]{3,2,1,0:T(8,128)(2,1)}, u32[]{:S(2)}) copy-start(bf16[1,2,128,2688]{3,2,1,0:T(8,128)(2,1)} %all-gather.3.cloned.1.call-done) | copy-start | bytes 4128772
  154.9 96.2 %reduce-scatter.7.cloned.1.call-start = ((), (), s32[]{:S(2)}) async-start(), calls=%async_computation.8 | async-start | bytes 774144 | tf_op jit(solution)/shard_map/reduce_scatter | solution.py:32
  155.1 0.5 copy-start.9
  189.5 6.4 %collective-permute-start = (bf16[16,2688]{1,0:T(8,128)(2,1)S(1)}, bf16[16,2688]{1,0:T(8,128)(2,1)S(1)}, u32[]{:S(2)}, u32[]{:S(2)}) collective-permute-start(bf16[16,2688]{1,0:T(8,128)(2,1)S(1)} %fusion.47), channel_id=1, source_target_pairs={{8,0},{16,8},{24,16},{0,24},{9,1},{17,9},{25,17},{1,25},{10,2},{18... | collective-permute-start | bytes 258056 | tf_op jit(solution)/shard_map/ppermute | solution.py:13
  215.3 0.7 copy-start.4
  221.6 101.3 %reduce-scatter.9.cloned.1.call-start = ((), (), s32[]{:S(2)}) async-start(), calls=%async_computation.9 | async-start | bytes 7741440 | tf_op jit(solution)/shard_map/reduce_scatter | solution.py:61
  221.9 1.9 copy-start.5
  221.9 1.9 copy-start.10
  228.3 1.1 copy-start.2
  228.4 167.3 %reduce-scatter.11.cloned.1.call-start = ((), (), s32[]{:S(2)}) async-start(), calls=%async_computation.10 | async-start | bytes 7741440 | tf_op jit(solution)/shard_map/reduce_scatter | solution.py:64
  235.8 0.7 copy-start.11
  235.8 16.4 %copy-start.7 = (f32[2688]{0:T(1024)S(1)}, f32[2688]{0:T(1024)}, u32[]{:S(2)}) copy-start(f32[2688]{0:T(1024)} %get-tuple-element.6) | copy-start | bytes 32260
Sparse Core Ops, SparseCore 0:
  9.6 31.9 all-gather.2
  43.5 101.8 all-gather.4
  155.0 31.7 reduce-scatter.4
  221.8 29.3 reduce-scatter.6
  254.6 68.2 reduce-scatter.8
  326.4 69.2 reduce-scatter.10
